TPU v7x, 128 devices: a whole 4x4x4 slice. The times are simulated.
128 devices in a mesh: group: 2 (over y_hi), win: 16 (over x, y_lo, core), mp: 4 (over z).
Axes of the slice: x: 4, y: 4 (y_hi: 2, y_lo: 2; y = y_hi * 2 + y_lo), z: 4, core: 2. Of those that a mesh axis runs over, the one named last changes fastest.
Arguments:
- tokens: bfloat16 [2, 4096, 4096], P('group', 'win', 'mp'), may hold values from -7 to 7, as said below
- proj: bfloat16 [2, 4096, 4096], P('group', None, 'mp'), may hold values from -1 to 1, as said below
- cotangent: bfloat16 [4096, 4096], P('win', 'mp'), may hold values from -6 to 6
- counts: int32 [16], P('win'), may hold values from 64 to 256, as said below
- frames: int32 [4096], P('win'), may hold values from 0 to 3, as said below
Outputs:
- input_grads: bfloat16 [2, 4096, 4096], P('group', 'win', 'mp')
- weight_grads: float32 [2, 4096, 4096], P('group', 'win', 'mp')
Inputs may be any that keep to these rules, and one draw needn't show every extreme that they name: Every value lies within the range; proj slot 0 entries scale as 1 / sqrt(1024), slot 1 as 1 / sqrt(4096). `tokens`: finite values. `counts`: some window has all 256 slots live and some window exactly 64. Each window has a token that sees only the first frame and one that sees all frames.
All inputs are finite; a program needn't handle non-finite values.
Results may differ from a plain program's by a relative error of at most 0.015.
The roundings to bfloat16 on the way count: a program that leaves them out, or rounds other values in their place, can miss the bound.
Values may be sent and summed in bfloat16 or wider, within the bound.
A program may use at most 192 MiB of HBM per device.

v0:
```python
import jax
import jax.numpy as jnp
from jax import lax
from jax.sharding import PartitionSpec as P

DV = 1024
HEAD_DIM = 128
FRAMES = 4


def from_behind(shard, axis, by):
    devices = lax.axis_size(axis)
    pairs = [(i, i + by) for i in range(devices) if 0 <= i + by < devices]
    return lax.ppermute(shard, axis, pairs)


def one_head(head_items, allowed):
    queries, key_rows, value_rows, upstream = head_items
    factor = HEAD_DIM ** (-0.5)
    scores = jnp.einsum("qd,kd->qk", queries, key_rows, preferred_element_type=jnp.float32) * factor
    scores = jnp.where(allowed, scores, -1e30)
    top_score = jnp.max(scores, axis=-1, keepdims=True)
    shifted = jnp.exp(scores - top_score)
    attention = shifted / jnp.sum(shifted, axis=-1, keepdims=True)
    rounded = attention.astype(jnp.bfloat16)
    value_grad = jnp.einsum(
        "qk,qd->kd", rounded, upstream, preferred_element_type=jnp.float32
    ).astype(jnp.bfloat16)
    attn_grad = jnp.einsum("qd,kd->qk", upstream, value_rows, preferred_element_type=jnp.float32)
    score_grad = (
        attention * (attn_grad - jnp.sum(attention * attn_grad, axis=-1, keepdims=True)) * factor
    )
    score_grad = score_grad.astype(jnp.bfloat16)
    query_grad = jnp.einsum(
        "qk,kd->qd", score_grad, key_rows, preferred_element_type=jnp.float32
    ).astype(jnp.bfloat16)
    key_grad = jnp.einsum(
        "qk,qd->kd", score_grad, queries, preferred_element_type=jnp.float32
    ).astype(jnp.bfloat16)
    return (query_grad, key_grad, value_grad)


def head_grads(queries, key_rows, value_rows, upstream, allowed):
    head_count = queries.shape[1] // HEAD_DIM

    def split_heads(array):
        return array.reshape(array.shape[0], head_count, HEAD_DIM).transpose(1, 0, 2)

    def merge_heads(array):
        return array.transpose(1, 0, 2).reshape(array.shape[1], head_count * HEAD_DIM)

    def per_head(head_items):
        return one_head(head_items, allowed)

    query_grad, key_grad, value_grad = lax.map(
        per_head,
        (
            split_heads(queries),
            split_heads(key_rows),
            split_heads(value_rows),
            split_heads(upstream),
        ),
    )
    return (merge_heads(query_grad), merge_heads(key_grad), merge_heads(value_grad))


def local(tokens, proj, cotangent, counts, frames):
    group_index = lax.axis_index("group")
    is_video = group_index == 0
    local_rows = tokens[0]
    weight = proj[0]
    row_count = local_rows.shape[0]
    columns = weight.shape[1]
    full_width = weight.shape[0]
    video_rows = row_count * full_width // DV
    gathered = lax.all_gather(local_rows, "mp", axis=1, tiled=True)
    features = gathered.reshape(video_rows, DV)
    w_key = weight[:DV]
    w_value = weight[DV : 2 * DV]

    def video_front():
        key_rows = jnp.dot(features, w_key, preferred_element_type=jnp.float32).astype(jnp.bfloat16)
        value_rows = jnp.dot(features, w_value, preferred_element_type=jnp.float32).astype(
            jnp.bfloat16
        )
        return (
            jnp.concatenate([key_rows, value_rows], 1),
            jnp.zeros((row_count, columns), jnp.bfloat16),
        )

    def neural_front():
        queries = jnp.dot(gathered, weight, preferred_element_type=jnp.float32).astype(jnp.bfloat16)
        return (jnp.zeros((video_rows, 2 * columns), jnp.bfloat16), queries)

    outgoing, queries = lax.cond(is_video, video_front, neural_front)
    arrived = from_behind(outgoing, "group", 1)
    key_rows = arrived[:, :columns]
    value_rows = arrived[:, columns:]
    live_rows = lax.iota(jnp.int32, row_count) < counts[0]
    upstream = jnp.where(live_rows[:, None], cotangent, jnp.zeros_like(cotangent))
    key_frame = lax.iota(jnp.int32, video_rows) // (video_rows // FRAMES)
    allowed = key_frame[None, :] <= frames[:, None]

    def attend():
        return head_grads(queries, key_rows, value_rows, upstream, allowed)

    def neural_input(query_grad):
        return jnp.dot(query_grad, weight.T, preferred_element_type=jnp.float32)

    def neural_weight(query_grad):
        return jnp.dot(gathered.T, query_grad, preferred_element_type=jnp.float32)

    def neural_all():
        query_grad, key_grad, value_grad = attend()
        return (
            jnp.concatenate([key_grad, value_grad], 1),
            query_grad,
            neural_input(query_grad),
            neural_weight(query_grad),
        )

    def video_wait_all():
        return (
            jnp.zeros((video_rows, 2 * columns), jnp.bfloat16),
            jnp.zeros((row_count, columns), jnp.bfloat16),
            jnp.zeros((row_count, full_width), jnp.float32),
            jnp.zeros((full_width, columns), jnp.float32),
        )

    returning, query_grad, early_input, early_weight = lax.cond(
        is_video, video_wait_all, neural_all
    )
    returned = from_behind(returning, "group", -1)

    def video_back():
        key_grad = returned[:, :columns]
        value_grad = returned[:, columns:]
        feature_part = jnp.dot(key_grad, w_key.T, preferred_element_type=jnp.float32)
        feature_part = feature_part + jnp.dot(
            value_grad, w_value.T, preferred_element_type=jnp.float32
        )
        feature_part = feature_part.reshape(row_count, full_width)
        weight_part = jnp.concatenate(
            [
                jnp.dot(features.T, key_grad, preferred_element_type=jnp.float32),
                jnp.dot(features.T, value_grad, preferred_element_type=jnp.float32),
                jnp.zeros((full_width - 2 * DV, columns), jnp.float32),
            ],
            0,
        )
        return (feature_part, weight_part)

    def neural_back():
        return (early_input, early_weight)

    input_part, weight_part = lax.cond(is_video, video_back, neural_back)
    summed = lax.psum_scatter(
        input_part.astype(jnp.bfloat16), "mp", scatter_dimension=1, tiled=True
    ).astype(jnp.float32)
    residual = jnp.where(is_video, jnp.zeros_like(summed), cotangent.astype(jnp.float32))
    input_grads = (summed + residual).astype(jnp.bfloat16)
    weight_grads = lax.psum_scatter(weight_part, "win", scatter_dimension=0, tiled=True)
    return (input_grads[None], weight_grads[None])


def solution(mesh):
    return jax.shard_map(
        local,
        mesh=mesh,
        in_specs=(
            P("group", "win", "mp"),
            P("group", None, "mp"),
            P("win", "mp"),
            P("win"),
            P("win"),
        ),
        out_specs=(P("group", "win", "mp"), P("group", "win", "mp")),
        check_vma=False,
    )
```

profile of v0, /device:TPU:1, one launch (start us, length us, event | category | flops | bytes accessed | tf_op | source)
XLA Modules:
  0.0 590.1 jit_solution(15386314961577830210)
XLA Ops:
  7.2 0.0 all-gather.3.cloned.1.call-start
  7.2 0.7 all-gather.3.cloned.1.call-update
  7.9 0.0 reduce-scatter.3.cloned.1.call-start
  8.0 4.7 slice_bitcast_fusion
  12.7 31.3 %all-gather.3.cloned.1.call-done = bf16[1,256,4096]{2,1,0:T(8,128)(2,1)} async-done(((bf16[1,256,1024]{2,1,0:T(8,128)(2,1)}), bf16[1,256,4096]{2,1,0:T(8,128)(2,1)}) %all-gather.3.cloned.1.call-update) | async-done | bytes 2097168 | tf_op jit(solution)/shard_map/all_gather | solution.py:76
  44.0 4.5 reshape.55
  48.5 8.5 %conditional.3 = (bf16[1024,2048]{0,1:T(8,128)(2,1)S(1)}, bf16[256,1024]{1,0:T(8,128)(2,1)}) conditional(s32[]{:T(128)} %convert_element_type.41, (bf16[256,4096]{1,0:T(8,128)(2,1)S(1)}, bf16[4096,1024]{1,0:T(8,128)(2,1)}) %tuple.116, (bf16[1024,1024]{1,0:T(8,128)(2,1)}, bf16[1024,1024]{1,0:T(8,128)(2,1)}, bf16[1024,1024]{1,0:T(8,128)(2,1)}) %tuple.68), branch_computations={%region_0.0_spmd, %region_1.0_spmd} | conditional | flops 4305453056 | bytes 38273096 | solution.py:95
  48.5 4.8 convolution_convert_fusion.2
  53.3 2.4 convolution_convert_fusion.1
  55.7 0.4 pad_maximum_fusion
  56.1 0.9 broadcast.66
  57.0 5.2 collective-permute-start
  62.2 87.3 %collective-permute-done = bf16[1024,2048]{0,1:T(8,128)(2,1)} collective-permute-done((bf16[1024,2048]{0,1:T(8,128)(2,1)S(1)}, bf16[1024,2048]{0,1:T(8,128)(2,1)}, u32[]{:S(2)}, u32[]{:S(2)}) %collective-permute-start) | collective-permute-done | bytes 4194336 | tf_op jit(solution)/shard_map/ppermute | solution.py:14
  149.5 8.8 %conditional.4 = (bf16[1024,2048]{1,0:T(8,128)(2,1)S(1)}, bf16[256,4096]{1,0:T(8,128)(2,1)S(1)}, f32[4096,1024]{0,1:T(8,128)}) conditional(s32[]{:T(128)} %convert_element_type.41, (bf16[256,1024]{1,0:T(8,128)(2,1)}, bf16[1024,2048]{0,1:T(8,128)(2,1)}, s32[1]{0:T(128)}, s32[256,1]{0,1:T(1,128)S(1)}, bf16[256,1024]{1,0:T(8,128)(2,1)S(1)}, ...), branch_computations={%region_2.8_spmd, %region_8.9_spmd} | conditional | flops 4644445696 | bytes 113604480 | solution.py:130
  149.7 0.2 broadcast.72
  149.9 0.5 broadcast.71
  150.4 7.9 %broadcast.73 = f32[4096,1024]{0,1:T(8,128)} broadcast(f32[]{:T(128)} %constant.80.clone), dimensions={} | broadcast | bytes 16777220 | tf_op jit(solution)/shard_map/broadcast.14
  158.3 1.3 collective-permute-start.1
  159.6 176.7 %collective-permute-done.1 = bf16[1024,2048]{1,0:T(8,128)(2,1)S(1)} collective-permute-done((bf16[1024,2048]{1,0:T(8,128)(2,1)S(1)}, bf16[1024,2048]{1,0:T(8,128)(2,1)S(1)}, u32[]{:S(2)}, u32[]{:S(2)}) %collective-permute-start.1) | collective-permute-done | bytes 4194336 | tf_op jit(solution)/shard_map/ppermute | solution.py:14
  336.3 34.7 %conditional.5 = (bf16[256,4096]{1,0:T(8,128)(2,1)}, f32[4096,1024]{1,0:T(8,128)}) conditional(s32[]{:T(128)} %convert_element_type.41, (bf16[256,4096]{1,0:T(8,128)(2,1)}, f32[4096,1024]{0,1:T(8,128)}) %tuple.118, (bf16[1024,2048]{1,0:T(8,128)(2,1)S(1)}, bf16[1024,1024]{1,0:T(8,128)(2,1)}, bf16[1024,1024]{1,0:T(8,128)(2,1)}, ...), branch_computations={%region_9.10_spmd, %region_10.11_spmd} | conditional | flops 8600420352 | bytes 115392640 | solution.py:156
  336.4 5.5 fusion.7
  341.9 3.7 convolution_add_fusion
  345.6 4.5 reshape.53
  350.1 6.2 %fusion.2 = f32[1024,1024]{1,0:T(8,128)} fusion(bf16[1024,1024]{1,0:T(8,128)(2,1)S(1)} %copy-done.4, bf16[1024,2048]{1,0:T(8,128)(2,1)} %copy-done.10), kind=kOutput, calls=%fused_computation.7 | convolution fusion | flops 2147483648 | bytes 8388608 | tf_op jit(solution)/shard_map/cond/branch_1_fun/dot_general | solution.py:146
  356.3 4.4 fusion.5
  360.7 10.3 %maximum_maximum_fusion = f32[4096,1024]{1,0:T(8,128)} fusion(f32[1024,1024]{1,0:T(8,128)} %fusion.2, f32[1024,1024]{1,0:T(8,128)} %fusion.5, f32[4096]{0:T(1024)S(1)} %pad.4.clone), kind=kLoop, calls=%fused_computation.5 | loop fusion | flops 8388608 | bytes 25182208 | tf_op jit(solution)/shard_map/cond/branch_1_fun/concatenate | solution.py:143
  371.0 0.0 reduce-scatter.3.cloned.1.call-update
  371.0 0.0 reduce-scatter.5.cloned.1.call-start
  371.1 0.7 reduce-scatter.5.cloned.1.call-update
  371.8 28.4 %reduce-scatter.3.cloned.1.call-done = bf16[256,1024]{1,0:T(8,128)(2,1)} async-done(((bf16[256,4096]{1,0:T(8,128)(2,1)}), bf16[256,1024]{1,0:T(8,128)(2,1)}) %reduce-scatter.3.cloned.1.call-update) | async-done | bytes 524304 | tf_op jit(solution)/shard_map/reduce_scatter | solution.py:157
  400.2 2.0 fusion.39
  402.2 181.4 %reduce-scatter.5.cloned.1.call-done = f32[256,1024]{1,0:T(8,128)} async-done(((f32[4096,1024]{1,0:T(8,128)}), f32[256,1024]{1,0:T(8,128)}) %reduce-scatter.5.cloned.1.call-update) | async-done | bytes 1048592 | tf_op jit(solution)/shard_map/reduce_scatter | solution.py:162
  (24 shorter events, 0.1 us)
Async XLA Ops:
  7.2 36.8 %all-gather.3.cloned.1.call-start = ((), (), s32[]{:S(2)}) async-start(), calls=%async_computation.4 | async-start | bytes 2621440 | tf_op jit(solution)/shard_map/all_gather | solution.py:76
  7.9 392.3 %reduce-scatter.3.cloned.1.call-start = ((), (), s32[]{:S(2)}) async-start(), calls=%async_computation.2 | async-start | bytes 2621440 | tf_op jit(solution)/shard_map/reduce_scatter | solution.py:157
  44.0 4.5 copy-start
  48.5 101.0 %copy-start.6 = (bf16[256,1024]{1,0:T(8,128)(2,1)S(1)}, bf16[256,1024]{1,0:T(8,128)(2,1)}, u32[]{:S(2)}) copy-start(bf16[256,1024]{1,0:T(8,128)(2,1)} %param.15) | copy-start | bytes 1572868
  48.5 101.0 %copy-start.12 = (s32[256]{0:T(256)S(1)}, s32[256]{0:T(256)}, u32[]{:S(2)}) copy-start(s32[256]{0:T(256)} %param.17) | copy-start | bytes 3076
  48.5 4.8 copy-start.3
  48.5 4.8 copy-start.7
  57.0 92.5 %collective-permute-start = (bf16[1024,2048]{0,1:T(8,128)(2,1)S(1)}, bf16[1024,2048]{0,1:T(8,128)(2,1)}, u32[]{:S(2)}, u32[]{:S(2)}) collective-permute-start(bf16[1024,2048]{0,1:T(8,128)(2,1)S(1)} %get-tuple-element.207), channel_id=1, source_target_pairs={{0,64},{1,65},{2,66},{3,67},{4,68},{5,69},{6,70},{7,71},{8,72},{9,... | collective-permute-start | bytes 12582920 | tf_op jit(solution)/shard_map/ppermute | solution.py:14
  158.3 178.0 %copy-start.5 = (bf16[256,4096]{1,0:T(8,128)(2,1)}, bf16[256,4096]{1,0:T(8,128)(2,1)S(1)}, u32[]{:S(2)}) copy-start(bf16[256,4096]{1,0:T(8,128)(2,1)S(1)} %get-tuple-element.208) | copy-start | bytes 6291460
  158.3 178.0 %collective-permute-start.1 = (bf16[1024,2048]{1,0:T(8,128)(2,1)S(1)}, bf16[1024,2048]{1,0:T(8,128)(2,1)S(1)}, u32[]{:S(2)}, u32[]{:S(2)}) collective-permute-start(bf16[1024,2048]{1,0:T(8,128)(2,1)S(1)} %get-tuple-element.210), channel_id=1, source_target_pairs={{64,0},{65,1},{66,2},{67,3},{68,4},{69,5},{70,6},{71,7},{72,8},{73... | collective-permute-start | bytes 12582920 | tf_op jit(solution)/shard_map/ppermute | solution.py:14
  336.3 5.5 copy-start.10
  336.3 5.5 copy-start.8
  345.6 4.5 copy-start.4
  350.1 6.2 %copy-start.11 = (bf16[1024,2048]{1,0:T(8,128)(2,1)S(1)}, bf16[1024,2048]{1,0:T(8,128)(2,1)}, u32[]{:S(2)}) copy-start(bf16[1024,2048]{1,0:T(8,128)(2,1)} %copy-done.10) | copy-start | bytes 12582916 | tf_op jit(solution)/shard_map/cond
  371.0 212.6 %reduce-scatter.5.cloned.1.call-start = ((), (), s32[]{:S(2)}) async-start(), calls=%async_computation.3 | async-start | bytes 17825792 | tf_op jit(solution)/shard_map/reduce_scatter | solution.py:162
Sparse Core Ops, SparseCore 0:
  9.7 34.2 all-gather.2
  371.2 28.9 reduce-scatter.2
  403.3 180.2 reduce-scatter.4
where the time goes:
time: 592 us; the launch traced here: 590 us
  waiting for transfers between devices  506 us (85%)
  matrix products  26.9 us (5%)
  local copies, waits for them, and re-layouts  23.3 us (4%)
  between operations  13.8 us (2%)
  other arithmetic  12.8 us (2%)
  starting transfers between devices  6.59 us (1%)
    ppermute x2, waiting for transfers between devices, from_behind(): return lax.ppermute(shard, axis, pairs)  264 us
    reduce_scatter x1, waiting for transfers between devices, local(): lax.psum_scatter(weight_part, 'win', scatter_dimension=0, tiled=True)  181 us
    all_gather x1, waiting for transfers between devices, local(): gathered = lax.all_gather(local_rows, 'mp', axis=1, tiled=True)  31.3 us
    reduce_scatter x1, waiting for transfers between devices, local(): lax.psum_scatter(input_part.astype(jnp.bfloat16), 'mp', scatter_dimension...  28.4 us
  transfers between devices with their start and end apart: 5, of which 5 were waited for; matrix products, arithmetic and copies ran while one was open for 1% of the time, Pallas kernels for 0%

commit v1 on v0

--- a/solution.py
+++ b/solution.py
@@ -73,7 +73,12 @@
     columns = weight.shape[1]
     full_width = weight.shape[0]
     video_rows = row_count * full_width // DV
-    gathered = lax.all_gather(local_rows, "mp", axis=1, tiled=True)
+    ring = [local_rows]
+    for hop in range(3):
+        ring.append(lax.ppermute(ring[-1], "mp", [(dev, (dev + 1) % 4) for dev in range(4)]))
+    gathered = jnp.roll(
+        jnp.concatenate(ring[::-1], axis=1), (lax.axis_index("mp") + 1) * ring[0].shape[1], axis=1
+    )
     features = gathered.reshape(video_rows, DV)
     w_key = weight[:DV]
     w_value = weight[DV : 2 * DV]

time: 592 us -> 593 us (level)
    ppermute x0 -> x3, waiting for transfers between devices: none -> 35.1 us  [local(): lax.ppermute(ring[-1], 'mp', [(dev, (dev + 1) % 4) for dev in range(4)])]
    all_gather x1 -> x0, waiting for transfers between devices: 31.3 us -> none  [local(): gathered = lax.all_gather(local_rows, 'mp', axis=1, tiled=True)]
  transfers between devices with their start and end apart: 5 -> 7, of which waited for: 5 -> 7; matrix products, arithmetic and copies ran while one was open for 1% -> 1% of each run, Pallas kernels for 0% -> 0%
where the time goes in v1:
time: 593 us; the launch traced here: 591 us
  waiting for transfers between devices  506 us (85%)
  matrix products  26.9 us (5%)
  local copies, waits for them, and re-layouts  21.8 us (4%)
  between operations  14.1 us (2%)
  other arithmetic  12.8 us (2%)
  starting transfers between devices  9.29 us (2%)
    ppermute x2, waiting for transfers between devices, from_behind(): return lax.ppermute(shard, axis, pairs)  259 us
    reduce_scatter x1, waiting for transfers between devices, local(): lax.psum_scatter(weight_part, 'win', scatter_dimension=0, tiled=True)  181 us
    ppermute x3, waiting for transfers between devices, local(): lax.ppermute(ring[-1], 'mp', [(dev, (dev + 1) % 4) for dev in range(4)])  35.1 us
    reduce_scatter x1, waiting for transfers between devices, local(): lax.psum_scatter(input_part.astype(jnp.bfloat16), 'mp', scatter_dimension...  29.7 us
  transfers between devices with their start and end apart: 7, of which 7 were waited for; matrix products, arithmetic and copies ran while one was open for 1% of the time, Pallas kernels for 0%

profile of v1, /device:TPU:1, one launch (start us, length us, event | category | flops | bytes accessed | tf_op | source)
XLA Modules:
  0.0 591.3 jit_solution(9501317238395307287)
XLA Ops:
  7.2 2.5 collective-permute-start
  9.7 14.0 %collective-permute-done = bf16[256,1024]{1,0:T(8,128)(2,1)S(1)} collective-permute-done((bf16[256,1024]{1,0:T(8,128)(2,1)}, bf16[256,1024]{1,0:T(8,128)(2,1)S(1)}, u32[]{:S(2)}, u32[]{:S(2)}) %collective-permute-start) | collective-permute-done | bytes 524320 | tf_op jit(solution)/shard_map/ppermute | solution.py:78
  23.7 13.4 %collective-permute-done.1 = bf16[256,1024]{1,0:T(8,128)(2,1)S(1)} collective-permute-done((bf16[256,1024]{1,0:T(8,128)(2,1)S(1)}, bf16[256,1024]{1,0:T(8,128)(2,1)S(1)}, u32[]{:S(2)}, u32[]{:S(2)}) %collective-permute-start.1) | collective-permute-done | bytes 524320 | tf_op jit(solution)/shard_map/ppermute | solution.py:78
  37.1 4.8 slice_bitcast_fusion
  41.9 7.7 %collective-permute-done.2 = bf16[256,1024]{1,0:T(8,128)(2,1)S(1)} collective-permute-done((bf16[256,1024]{1,0:T(8,128)(2,1)S(1)}, bf16[256,1024]{1,0:T(8,128)(2,1)S(1)}, u32[]{:S(2)}, u32[]{:S(2)}) %collective-permute-start.2) | collective-permute-done | bytes 524320 | tf_op jit(solution)/shard_map/ppermute | solution.py:78
  50.0 0.1 constant_dynamic-slice_fusion
  50.1 2.6 reshape.55
  52.7 8.5 %conditional.3 = (bf16[1024,2048]{0,1:T(8,128)(2,1)S(1)}, bf16[256,1024]{1,0:T(8,128)(2,1)}) conditional(s32[]{:T(128)} %convert_element_type.41, (bf16[256,4096]{1,0:T(8,128)(2,1)S(1)}, bf16[4096,1024]{1,0:T(8,128)(2,1)}) %tuple.107, (bf16[1024,1024]{1,0:T(8,128)(2,1)}, bf16[1024,1024]{1,0:T(8,128)(2,1)}, bf16[1024,1024]{1,0:T(8,128)(2,1)}) %tuple.63), branch_computations={%region_0.1_spmd, %region_1.2_spmd} | conditional | flops 4305453056 | bytes 38273096 | solution.py:100
  52.7 4.8 convolution_convert_fusion.2
  57.5 2.4 convolution_convert_fusion.1
  59.9 0.4 pad_maximum_fusion
  60.3 0.9 broadcast.68
  61.2 5.4 collective-permute-start.3
  66.6 84.8 %collective-permute-done.3 = bf16[1024,2048]{0,1:T(8,128)(2,1)} collective-permute-done((bf16[1024,2048]{0,1:T(8,128)(2,1)S(1)}, bf16[1024,2048]{0,1:T(8,128)(2,1)}, u32[]{:S(2)}, u32[]{:S(2)}) %collective-permute-start.3) | collective-permute-done | bytes 4194336 | tf_op jit(solution)/shard_map/ppermute | solution.py:14
  151.4 8.8 %conditional.4 = (bf16[1024,2048]{1,0:T(8,128)(2,1)S(1)}, bf16[256,4096]{1,0:T(8,128)(2,1)S(1)}, f32[4096,1024]{0,1:T(8,128)}) conditional(s32[]{:T(128)} %convert_element_type.41, (bf16[256,1024]{1,0:T(8,128)(2,1)}, bf16[1024,2048]{0,1:T(8,128)(2,1)}, s32[1]{0:T(128)}, s32[256,1]{0,1:T(1,128)S(1)}, bf16[256,1024]{1,0:T(8,128)(2,1)S(1)}, ...), branch_computations={%region_2.8_spmd, %region_8.9_spmd} | conditional | flops 4644445696 | bytes 113604480 | solution.py:135
  151.6 0.2 broadcast.75
  151.9 0.5 broadcast.74
  152.4 7.9 %broadcast.76 = f32[4096,1024]{0,1:T(8,128)} broadcast(f32[]{:T(128)} %constant.100.clone), dimensions={} | broadcast | bytes 16777220 | tf_op jit(solution)/shard_map/broadcast.14
  160.3 1.3 collective-permute-start.4
  161.5 174.3 %collective-permute-done.4 = bf16[1024,2048]{1,0:T(8,128)(2,1)S(1)} collective-permute-done((bf16[1024,2048]{1,0:T(8,128)(2,1)S(1)}, bf16[1024,2048]{1,0:T(8,128)(2,1)S(1)}, u32[]{:S(2)}, u32[]{:S(2)}) %collective-permute-start.4) | collective-permute-done | bytes 4194336 | tf_op jit(solution)/shard_map/ppermute | solution.py:14
  335.9 34.7 %conditional.5 = (bf16[256,4096]{1,0:T(8,128)(2,1)}, f32[4096,1024]{1,0:T(8,128)}) conditional(s32[]{:T(128)} %convert_element_type.41, (bf16[256,4096]{1,0:T(8,128)(2,1)}, f32[4096,1024]{0,1:T(8,128)}) %tuple.109, (bf16[1024,2048]{1,0:T(8,128)(2,1)S(1)}, bf16[1024,1024]{1,0:T(8,128)(2,1)}, bf16[1024,1024]{1,0:T(8,128)(2,1)}, ...), branch_computations={%region_9.10_spmd, %region_10.11_spmd} | conditional | flops 8600420352 | bytes 115392640 | solution.py:161
  335.9 5.5 fusion.7
  341.4 3.7 convolution_add_fusion
  345.1 4.5 reshape.53
  349.6 6.2 %fusion.2 = f32[1024,1024]{1,0:T(8,128)} fusion(bf16[1024,1024]{1,0:T(8,128)(2,1)S(1)} %copy-done.3, bf16[1024,2048]{1,0:T(8,128)(2,1)} %copy-done.10), kind=kOutput, calls=%fused_computation.7 | convolution fusion | flops 2147483648 | bytes 8388608 | tf_op jit(solution)/shard_map/cond/branch_1_fun/dot_general | solution.py:151
  355.8 4.4 fusion.5
  360.2 10.3 %maximum_maximum_fusion = f32[4096,1024]{1,0:T(8,128)} fusion(f32[1024,1024]{1,0:T(8,128)} %fusion.2, f32[1024,1024]{1,0:T(8,128)} %fusion.5, f32[4096]{0:T(1024)S(1)} %pad.4.clone), kind=kLoop, calls=%fused_computation.5 | loop fusion | flops 8388608 | bytes 25182208 | tf_op jit(solution)/shard_map/cond/branch_1_fun/concatenate | solution.py:148
  370.6 0.0 reduce-scatter.5.cloned.1.call-start
  370.6 0.7 reduce-scatter.5.cloned.1.call-update
  371.4 29.7 %reduce-scatter.3.cloned.1.call-done = bf16[256,1024]{1,0:T(8,128)(2,1)} async-done(((bf16[256,4096]{1,0:T(8,128)(2,1)}), bf16[256,1024]{1,0:T(8,128)(2,1)}) %reduce-scatter.3.cloned.1.call-update) | async-done | bytes 524304 | tf_op jit(solution)/shard_map/reduce_scatter | solution.py:162
  401.0 2.0 fusion.39
  403.1 181.4 %reduce-scatter.5.cloned.1.call-done = f32[256,1024]{1,0:T(8,128)} async-done(((f32[4096,1024]{1,0:T(8,128)}), f32[256,1024]{1,0:T(8,128)}) %reduce-scatter.5.cloned.1.call-update) | async-done | bytes 1048592 | tf_op jit(solution)/shard_map/reduce_scatter | solution.py:167
  (36 shorter events, 0.4 us)
Async XLA Ops:
  7.2 393.9 %reduce-scatter.3.cloned.1.call-start = ((), (), s32[]{:S(2)}) async-start(), calls=%async_computation.2 | async-start | bytes 2621440 | tf_op jit(solution)/shard_map/reduce_scatter | solution.py:162
  7.2 16.5 %collective-permute-start = (bf16[256,1024]{1,0:T(8,128)(2,1)}, bf16[256,1024]{1,0:T(8,128)(2,1)S(1)}, u32[]{:S(2)}, u32[]{:S(2)}) collective-permute-start(bf16[256,1024]{1,0:T(8,128)(2,1)} %bitcast.130), channel_id=1, source_target_pairs={{0,1},{1,2},{2,3},{3,0},{4,5},{5,6},{6,7},{7,4},{8,9},{9,10},{10,1... | collective-permute-start | bytes 1572872 | tf_op jit(solution)/shard_map/ppermute | solution.py:78
  23.7 13.4 %collective-permute-start.1 = (bf16[256,1024]{1,0:T(8,128)(2,1)S(1)}, bf16[256,1024]{1,0:T(8,128)(2,1)S(1)}, u32[]{:S(2)}, u32[]{:S(2)}) collective-permute-start(bf16[256,1024]{1,0:T(8,128)(2,1)S(1)} %collective-permute-done), channel_id=1, source_target_pairs={{0,1},{1,2},{2,3},{3,0},{4,5},{5,6},{6,7},{7,4},{8,9},{9,10},{10,1... | collective-permute-start | bytes 1572872 | tf_op jit(solution)/shard_map/ppermute | solution.py:78
  37.1 12.5 %collective-permute-start.2 = (bf16[256,1024]{1,0:T(8,128)(2,1)S(1)}, bf16[256,1024]{1,0:T(8,128)(2,1)S(1)}, u32[]{:S(2)}, u32[]{:S(2)}) collective-permute-start(bf16[256,1024]{1,0:T(8,128)(2,1)S(1)} %collective-permute-done.1), channel_id=1, source_target_pairs={{0,1},{1,2},{2,3},{3,0},{4,5},{5,6},{6,7},{7,4},{8,9},{9,10},{10,1... | collective-permute-start | bytes 1572872 | tf_op jit(solution)/shard_map/ppermute | solution.py:78
  41.9 7.8 %copy-start.5 = (bf16[1,256,1024]{2,1,0:T(8,128)(2,1)S(1)}, bf16[1,256,1024]{2,1,0:T(8,128)(2,1)}, u32[]{:S(2)}) copy-start(bf16[1,256,1024]{2,1,0:T(8,128)(2,1)} %param.13) | copy-start | bytes 1572868
  52.7 98.7 %copy-start.6 = (bf16[256,1024]{1,0:T(8,128)(2,1)S(1)}, bf16[256,1024]{1,0:T(8,128)(2,1)}, u32[]{:S(2)}) copy-start(bf16[256,1024]{1,0:T(8,128)(2,1)} %param.15) | copy-start | bytes 1572868
  52.7 98.7 %copy-start.12 = (s32[256]{0:T(256)S(1)}, s32[256]{0:T(256)}, u32[]{:S(2)}) copy-start(s32[256]{0:T(256)} %param.17) | copy-start | bytes 3076
  52.7 4.8 copy-start.2
  52.7 4.8 copy-start.7
  61.2 90.2 %collective-permute-start.3 = (bf16[1024,2048]{0,1:T(8,128)(2,1)S(1)}, bf16[1024,2048]{0,1:T(8,128)(2,1)}, u32[]{:S(2)}, u32[]{:S(2)}) collective-permute-start(bf16[1024,2048]{0,1:T(8,128)(2,1)S(1)} %get-tuple-element.211), channel_id=1, source_target_pairs={{0,64},{1,65},{2,66},{3,67},{4,68},{5,69},{6,70},{7,71},{8,72},{9,... | collective-permute-start | bytes 12582920 | tf_op jit(solution)/shard_map/ppermute | solution.py:14
  160.3 175.6 %copy-start.4 = (bf16[256,4096]{1,0:T(8,128)(2,1)}, bf16[256,4096]{1,0:T(8,128)(2,1)S(1)}, u32[]{:S(2)}) copy-start(bf16[256,4096]{1,0:T(8,128)(2,1)S(1)} %get-tuple-element.212) | copy-start | bytes 6291460
  160.3 175.6 %collective-permute-start.4 = (bf16[1024,2048]{1,0:T(8,128)(2,1)S(1)}, bf16[1024,2048]{1,0:T(8,128)(2,1)S(1)}, u32[]{:S(2)}, u32[]{:S(2)}) collective-permute-start(bf16[1024,2048]{1,0:T(8,128)(2,1)S(1)} %get-tuple-element.214), channel_id=1, source_target_pairs={{64,0},{65,1},{66,2},{67,3},{68,4},{69,5},{70,6},{71,7},{72,8},{73... | collective-permute-start | bytes 12582920 | tf_op jit(solution)/shard_map/ppermute | solution.py:14
  335.9 5.5 copy-start.10
  335.9 5.5 copy-start.8
  345.1 4.5 copy-start.3
  349.6 6.2 %copy-start.11 = (bf16[1024,2048]{1,0:T(8,128)(2,1)S(1)}, bf16[1024,2048]{1,0:T(8,128)(2,1)}, u32[]{:S(2)}) copy-start(bf16[1024,2048]{1,0:T(8,128)(2,1)} %copy-done.10) | copy-start | bytes 12582916 | tf_op jit(solution)/shard_map/cond
  370.6 213.9 %reduce-scatter.5.cloned.1.call-start = ((), (), s32[]{:S(2)}) async-start(), calls=%async_computation.3 | async-start | bytes 17825792 | tf_op jit(solution)/shard_map/reduce_scatter | solution.py:167
Sparse Core Ops, SparseCore 0:
  370.7 30.2 reduce-scatter.2
  404.1 180.2 reduce-scatter.4
